TPU v7x, 32 devices: a whole 2x2x4 slice. The times are simulated.
32 devices in a mesh: shot: 4 (over x, core), rcv: 8 (over z, y).
Axes of the slice: x: 2, y: 2, z: 4, core: 2. Of those that a mesh axis runs over, the one named last changes fastest.
Arguments:
- response: bfloat16 [128, 128, 64], P('shot', 'rcv'), may hold values from -0.0625 to 0.0625
- traces: bfloat16 [128, 64, 512], P('shot', 'rcv'), may hold values from -6 to 6
Outputs:
- multiples: bfloat16 [128, 64, 512], P('shot', 'rcv')
All inputs are finite; a program needn't handle non-finite values.
Results may differ from a plain program's by a relative error of at most 0.001.
Values may be sent and summed in bfloat16 or wider, within the bound.
A program may use at most 256 MiB of HBM per device.

v0:
```python
import functools

import jax
import jax.numpy as jnp
from jax import lax
from jax.experimental import pallas as pl
from jax.experimental.pallas import tpu as pltpu
from jax.sharding import PartitionSpec as P

MESH = pl.DeviceIdType.MESH
LANES = 128
WIDTH = 256


def put(ref, value):
    for t in range(value.shape[1] // LANES):
        ref[t] = value[:, t * LANES : (t + 1) * LANES]


def put_rows(ref, start, count, stride, value):
    for t in range(value.shape[1] // LANES):
        ref[t, pl.ds(start, count, stride=stride), :] = value[:, t * LANES : (t + 1) * LANES]


def get(ref):
    return jnp.concatenate([ref[t] for t in range(ref.shape[0])], axis=1)


def get_rows(ref, start, count, stride):
    return jnp.concatenate(
        [ref[t, pl.ds(start, count, stride=stride), :] for t in range(ref.shape[0])], axis=1
    )


def turn_response(response, b_ref, y_ref, h_ref):
    shots, rows_e, taps = response.shape
    per_tile = LANES // shots
    tiles = taps // per_tile
    b_ref[:, :taps] = response.astype(jnp.float32).reshape(shots * rows_e, taps)
    stacked = jnp.concatenate(
        [b_ref[pl.ds(k, shots, stride=rows_e), :] for k in range(rows_e)], axis=0
    )
    put(y_ref, stacked.T[:taps])
    by_tap = [get_rows(y_ref, m, tiles, per_tile) for m in range(per_tile)]
    for k in range(rows_e):
        h_ref[pl.ds(k, tiles, stride=rows_e), :] = jnp.concatenate(
            [v[:, k * shots : (k + 1) * shots] for v in by_tap], axis=1
        )
    return h_ref[...].astype(jnp.bfloat16)


def turn_traces(traces, phases, a_ref, z_ref, w_ref):
    rows_d, rcv, samples = traces.shape
    blocks = samples // phases
    put(a_ref, traces.astype(jnp.float32).reshape(rows_d * rcv, samples))
    stacked = jnp.concatenate([get_rows(a_ref, r, rows_d, rcv) for r in range(rcv)], axis=0)
    put(z_ref, stacked.T)
    by_phase = [get_rows(z_ref, v, blocks, phases) for v in range(phases)]
    for r in range(rcv):
        row = jnp.concatenate([z[:, r * rows_d : (r + 1) * rows_d] for z in by_phase], axis=1)
        put_rows(w_ref, r, blocks, rcv, row)
    return get(w_ref).astype(jnp.bfloat16)


def arrange(y_ref, o_ref, acc, z_ref, f_ref):
    shots, rcv, samples = o_ref.shape
    phases = WIDTH // shots
    blocks = samples // phases
    put(acc, y_ref[...].astype(jnp.float32))
    by_rcv = [get_rows(acc, r, blocks, rcv) for r in range(rcv)]
    for u in range(phases):
        row = jnp.concatenate([v[:, u * shots : (u + 1) * shots] for v in by_rcv], axis=1)
        put_rows(z_ref, u, blocks, phases, row)
    turned = get(z_ref).T
    for r in range(rcv):
        put_rows(f_ref, r, shots, rcv, turned[r * shots : (r + 1) * shots])
    o_ref[...] = get(f_ref).reshape(shots, rcv, samples).astype(jnp.bfloat16)


def predict(
    n_shot, n_rcv, chunks,
    response_hbm, traces_hbm, o_ref,
    response_ref, traces_ref, b_ref, y_ref, h_ref, a_ref, z_ref, w_ref,
    x_ref, g_ref, xland, gland, bands, even, odd, acc,
    load, xsend, xrecv, xfwd, gsend, grecv, gfwd,
):
    shots, rows_e, taps = response_ref.shape
    rows_d, rcv, samples = traces_ref.shape
    rows, width = x_ref.shape
    phases = WIDTH // shots
    per_tile = LANES // shots
    tiles = taps // per_tile
    pad = phases // per_tile
    history = taps // phases
    ratio = rows_d // rows_e
    head = history * rcv
    half = rows // 2
    outer_d, outer_e = n_shot // 2, n_rcv // 2
    me_d, me_e = lax.axis_index("shot"), lax.axis_index("rcv")
    in_d, in_e = lax.rem(me_d, 2), lax.rem(me_e, 2)
    out_d, out_e = me_d // 2, me_e // 2
    mate_d = out_d * 2 + 1 - in_d
    mate_e = out_e * 2 + 1 - in_e

    def at_d(step):
        return lax.rem(out_d + step + outer_d, outer_d) * 2 + in_d

    def at_e(step):
        return lax.rem(out_e + step + outer_e, outer_e) * 2 + in_e

    barrier = pltpu.get_barrier_semaphore()
    peers = [(mate_d, me_e), (me_d, mate_e)]
    peers += [(at_d(i), me_e) for i in range(1, outer_d)]
    peers += [(me_d, at_e(i)) for i in range(1, outer_e)]
    for peer in peers:
        pl.semaphore_signal(barrier, inc=1, device_id=peer, device_id_type=MESH)
    fetch_r = pltpu.make_async_copy(response_hbm, response_ref, load.at[0])
    fetch_t = pltpu.make_async_copy(traces_hbm, traces_ref, load.at[1])
    fetch_r.start()
    fetch_t.start()

    part = rows // chunks

    def xcopy(src, owner, c, send, peer):
        piece = pl.ds(c * part, part)
        return pltpu.make_async_remote_copy(
            src_ref=src.at[piece],
            dst_ref=xland.at[owner, piece],
            send_sem=send,
            recv_sem=xrecv.at[owner, c],
            device_id=peer,
            device_id_type=MESH,
        )

    def gcopy(src, owner, send, peer):
        return pltpu.make_async_remote_copy(
            src_ref=src,
            dst_ref=gland.at[owner],
            send_sem=send,
            recv_sem=grecv.at[owner],
            device_id=peer,
            device_id_type=MESH,
        )

    pending = []

    def go(copy):
        copy.start()
        pending.append(copy)

    fetch_r.wait()
    g_ref[...] = turn_response(response_ref[...], b_ref, y_ref, h_ref)
    pl.semaphore_wait(barrier, len(peers))
    order = sorted(range(1, outer_e), key=lambda i: abs(2 * i - outer_e))
    for i in order:
        go(gcopy(g_ref, me_e, gsend.at[i], (me_d, at_e(i))))
    go(gcopy(g_ref, me_e, gsend.at[0], (me_d, mate_e)))
    fetch_t.wait()
    span = samples // chunks
    for c in range(chunks + 1):
        if c < chunks:
            x_ref[pl.ds(c * part, part), :] = turn_traces(
                traces_ref[:, :, pl.ds(c * span, span)], phases, a_ref, z_ref, w_ref
            )
        if c > 0:
            for i in range(1, outer_d):
                go(xcopy(x_ref, me_d, c - 1, xsend.at[i, c - 1], (at_d(i), me_e)))
    for c in range(chunks):
        go(xcopy(x_ref, me_d, c, xsend.at[0, c], (mate_d, me_e)))

    blank = jnp.zeros((rows_e, LANES), jnp.bfloat16)

    def build(e, held):
        padded = [blank] * pad
        padded += [held[a * rows_e : (a + 1) * rows_e] for a in range(tiles)]
        padded += [blank] * (pad + 1)
        for a in range(tiles + 2 * pad):
            for q in range(per_tile):
                value = padded[a]
                if q > 0:
                    value = jnp.concatenate(
                        [padded[a][:, q * shots :], padded[a + 1][:, : q * shots]], axis=1
                    )
                bands[e, q, a] = value

    def place(owner, held, h):
        even[owner, pl.ds(head + h * half, half), :] = held
        odd[owner, pl.ds(head - rcv + h * half, half), :] = held

    def add(owner, h, first=False, last=False):
        left, right = [], []
        for v1 in range(history + 1):
            if v1 % 2 == 0:
                left.append(even[owner, pl.ds(h * half + v1 * rcv, half), :])
            else:
                left.append(odd[owner, pl.ds(h * half + (v1 - 1) * rcv, half), :])
            for v0 in range(phases):
                start = taps - v1 * phases - v0 + phases
                a, q = start // per_tile, start % per_tile
                for k in range(ratio):
                    e = owner * ratio + k
                    right.append(
                        jnp.concatenate([bands[e, q, a + n] for n in range(pad)], axis=1)
                    )
        total = jnp.dot(
            jnp.concatenate(left, axis=1),
            jnp.concatenate(right, axis=0),
            preferred_element_type=jnp.float32,
        )
        mine = pl.ds(h * half, half)
        if not first:
            total = acc[mine, :] + total
        if last:
            o_ref[mine, :] = total.astype(jnp.bfloat16)
        else:
            acc[mine, :] = total

    def forward_x(i, c):
        owner = at_d(-i)
        copy = xcopy(xland.at[owner], owner, c, xfwd.at[i, c], (mate_d, me_e))
        copy.wait_recv()
        go(copy)

    for d in range(n_shot):
        even[d, pl.ds(0, head), :] = jnp.zeros((head, width), jnp.bfloat16)
        odd[d, pl.ds(0, head), :] = jnp.zeros((head, width), jnp.bfloat16)
    for h in range(2):
        place(me_d, x_ref[pl.ds(h * half, half), :], h)
    build(me_e, g_ref[...])

    def arrived(owner):
        for c in range(chunks):
            xcopy(x_ref, owner, c, xsend.at[0, c], (mate_d, me_e)).wait_recv()

    def bring(owner):
        for h in range(2):
            place(owner, xland[owner, pl.ds(h * half, half), :], h)

    todo = [(i, c) for c in range(chunks) for i in range(1, outer_d)]
    for n in range(max(outer_e - 1, len(todo))):
        if n < len(todo):
            forward_x(*todo[n])
        if n < outer_e - 1:
            owner = at_e(-order[n])
            copy = gcopy(gland.at[owner], owner, gfwd.at[n], (me_d, mate_e))
            copy.wait_recv()
            go(copy)
        if n < outer_e - 1:
            build(owner, gland[owner])
    def meet(group):
        owner = group * 2 + 1 - in_e
        gcopy(g_ref, owner, gsend.at[0], (me_d, mate_e)).wait_recv()
        build(owner, gland[owner])

    meet(out_e)
    arrived(mate_d)
    bring(mate_d)
    for i in range(1, outer_d):
        bring(at_d(-i))
    for i in range(1, outer_d):
        owner = lax.rem(out_d - i + outer_d, outer_d) * 2 + 1 - in_d
        arrived(owner)
        bring(owner)

    for n, i in enumerate([0] + order):
        group = lax.rem(out_e - i + outer_e, outer_e)
        if n > 0:
            meet(group)
        if ratio == 2:
            for h in range(2):
                add(group, h, first=n == 0, last=n == outer_e - 1)
    if ratio != 2:
        for d in range(n_shot):
            for h in range(2):
                add(d, h, first=d == 0, last=d == n_shot - 1)
    for copy in pending:
        copy.wait_send()


def shards(n_shot, n_rcv, response, traces):
    shots, rows_e, taps = response.shape
    rows_d, rcv, samples = traces.shape
    phases = WIDTH // shots
    blocks = samples // phases
    per_tile = LANES // shots
    tiles = taps // per_tile
    pad = phases // per_tile
    rows = blocks * rcv
    width = phases * rows_d
    chunks = 4
    f32, bf16 = jnp.float32, jnp.bfloat16

    def tiled(height, across):
        return pltpu.VMEM((across // LANES, height, LANES), f32)

    vmem = pl.BlockSpec(memory_space=pltpu.VMEM)
    outer_d, outer_e = n_shot // 2, n_rcv // 2
    head = taps // phases * rcv
    dma = pltpu.SemaphoreType.DMA
    y = pl.pallas_call(
        functools.partial(predict, n_shot, n_rcv, chunks),
        out_shape=jax.ShapeDtypeStruct((rows, WIDTH), bf16),
        in_specs=[pl.BlockSpec(memory_space=pl.ANY)] * 2,
        out_specs=vmem,
        scratch_shapes=[
            pltpu.VMEM(response.shape, bf16),
            pltpu.VMEM(traces.shape, bf16),
            pltpu.VMEM((shots * rows_e, LANES), f32),
            tiled(taps, rows_e * shots),
            pltpu.VMEM((tiles * rows_e, LANES), f32),
            tiled(rows_d * rcv, samples // chunks),
            tiled(samples // chunks, rcv * rows_d),
            tiled(rows // chunks, width),
            pltpu.VMEM((rows, width), bf16),
            pltpu.VMEM((tiles * rows_e, LANES), bf16),
            pltpu.VMEM((n_shot, rows, width), bf16),
            pltpu.VMEM((n_rcv, tiles * rows_e, LANES), bf16),
            pltpu.VMEM((n_rcv, per_tile, tiles + 2 * pad, rows_e, LANES), bf16),
            pltpu.VMEM((n_shot, rows + head, width), bf16),
            pltpu.VMEM((n_shot, rows + head, width), bf16),
            pltpu.VMEM((rows, WIDTH), f32),
            dma((2,)),
            dma((outer_d, chunks)),
            dma((n_shot, chunks)),
            dma((outer_d, chunks)),
            dma((outer_e,)),
            dma((n_rcv,)),
            dma((outer_e,)),
        ],
        compiler_params=pltpu.CompilerParams(collective_id=0, has_side_effects=True),
    )(response, traces)
    return pl.pallas_call(
        arrange,
        out_shape=jax.ShapeDtypeStruct((shots, rcv, samples), bf16),
        in_specs=[vmem],
        out_specs=vmem,
        scratch_shapes=[
            tiled(rows, WIDTH),
            tiled(samples, rcv * shots),
            tiled(shots * rcv, samples),
        ],
    )(y)


def solution(mesh):
    placed = P("shot", "rcv", None)
    return jax.shard_map(
        functools.partial(shards, mesh.shape["shot"], mesh.shape["rcv"]),
        mesh=mesh, in_specs=(placed, placed), out_specs=placed, check_vma=False,
    )
```

profile of v0, /device:TPU:0, one launch (start us, length us, event | category | flops | bytes accessed | tf_op | source)
XLA Modules:
  0.0 20.7 jit_solution(4371774565217377020)
XLA Ops:
  0.0 18.4 %shard_map.28.y_ref = bf16[512,256]{1,0:T(8,128)(2,1)} custom-call(bf16[32,16,64]{2,1,0:T(8,128)(2,1)} %response_hbm.1, bf16[32,8,512]{2,1,0:T(8,128)(2,1)} %traces_hbm.1), custom_call_target="tpu_custom_call" | custom-call | tf_op jit(solution)/shard_map/pallas_call | solution.py:300
  18.4 2.4 %shard_map.29 = bf16[32,8,512]{2,1,0:T(8,128)(2,1)} custom-call(bf16[512,256]{1,0:T(8,128)(2,1)} %shard_map.28.y_ref), custom_call_target="tpu_custom_call" | custom-call | tf_op jit(solution)/shard_map/pallas_call | solution.py:332
where the time goes:
time: 20.9 us; the launch traced here: 20.7 us
  Pallas kernels  20.7 us (99%)
    pallas_call x1, Pallas kernels, shards(): pl.pallas_call(functools.partial(predict, n_shot, n_rcv, chunks), out_sha...  18.4 us
    pallas_call x1, Pallas kernels, shards(): pl.pallas_call(arrange, out_shape=jax.ShapeDtypeStruct((shots, rcv, sampl...  2.38 us

commit v1 on v0

--- a/solution.py
+++ b/solution.py
@@ -277,7 +277,7 @@
         copy.wait_send()
 
 
-def shards(n_shot, n_rcv, response, traces):
+def shards_general(n_shot, n_rcv, response, traces):
     shots, rows_e, taps = response.shape
     rows_d, rcv, samples = traces.shape
     phases = WIDTH // shots
@@ -342,6 +342,370 @@
     )(y)
 
 
+def swap_groups(rows, size):
+    lane = lax.broadcasted_iota(jnp.int32, rows[0].shape, 1) // size
+    step = 1
+    while step < len(rows):
+        keep = (lane // step) % 2 == 0
+        turned = list(rows)
+        for i in range(len(rows)):
+            if (i // step) % 2 == 0:
+                a, b = rows[i], rows[i + step]
+                turned[i] = jnp.where(keep, a, pltpu.roll(b, step * size, 1))
+                turned[i + step] = jnp.where(keep, pltpu.roll(a, LANES - step * size, 1), b)
+        rows = turned
+        step *= 2
+    return rows
+
+
+def lag_response(response, lags, y_ref, w_ref):
+    shots, rows_e, taps = response.shape
+    per_tile = LANES // rows_e
+    flat = response.reshape(shots * rows_e, taps)
+    row = lax.broadcasted_iota(jnp.int32, (taps, taps), 0)
+    col = lax.broadcasted_iota(jnp.int32, (taps, taps), 1)
+    put(y_ref, lax.dot_general(
+        (row == col).astype(jnp.bfloat16), flat, (((1,), (1,)), ((), ())),
+        preferred_element_type=jnp.float32,
+    ))
+    for tile in range(shots // per_tile):
+        rows = [y_ref[tile, pl.ds(j, taps // lags, stride=lags), :] for j in range(lags)]
+        for i, value in enumerate(swap_groups(rows, rows_e)):
+            w_ref[pl.ds(tile * per_tile + i, taps // lags, stride=shots), :] = value
+    return w_ref[...].astype(jnp.bfloat16)
+
+
+def later(tiles, lag):
+    if lag == 0:
+        return tiles
+    turned = [pltpu.roll(v, lag, 1) for v in tiles]
+    lane = lax.broadcasted_iota(jnp.int32, tiles[0].shape, 1)
+    before = [jnp.zeros_like(turned[0])] + turned[:-1]
+    return [jnp.where(lane >= lag, v, b) for v, b in zip(turned, before)]
+
+
+def delayed(x, lag):
+    if lag == 0:
+        return x
+    blank = jnp.zeros((x.shape[0], lag), x.dtype)
+    return jnp.concatenate([blank, x[:, : x.shape[1] - lag]], axis=1)
+
+
+def predict_line(
+    n_shot, n_rcv, lags, chunks,
+    response_hbm, traces_hbm, o_ref,
+    response_ref, y_ref, w_ref, gland, tland, a_ref, sh_ref, p_ref, f_ref,
+    load, sent, tmate, tpeer, tfar, gline, gside, gover, joined,
+):
+    shots, rows_e, taps = response_ref.shape
+    rows_d, rcv, samples = tland.shape[1:]
+    steps = taps // lags
+    length = n_rcv // 2
+    me_d, me_e = lax.axis_index("shot"), lax.axis_index("rcv")
+    in_d, in_e = lax.rem(me_d, 2), lax.rem(me_e, 2)
+    out_d, place = me_d // 2, me_e // 2
+    mate_d = me_d + 1 - 2 * in_d
+    mate_e = me_e + 1 - 2 * in_e
+    peer_d = lax.rem(me_d + 2, n_shot)
+    far_d = lax.rem(mate_d + 2, n_shot)
+    low_bit, high_bit = lax.rem(place, 2), place // 2
+    spots = [
+        place + (n % 2) * (1 - 2 * low_bit) + (n // 2) * (2 - 4 * high_bit)
+        for n in range(length)
+    ]
+    peers = [
+        ((mate_d, me_e), in_d == 1, 0),
+        ((peer_d, me_e), out_d == 1, 1),
+        ((me_d, mate_e), in_e == 1, 2),
+    ]
+    peers += [((me_d, 2 * spots[n] + in_e), spots[n] < place, 2 + n) for n in range(1, length)]
+
+    def hold(sem, count):
+        @pl.when(count > 0)
+        def _():
+            pl.semaphore_wait(sem, count)
+
+    barrier = pltpu.get_barrier_semaphore()
+    for peer, below, _ in peers:
+        @pl.when(jnp.logical_not(below))
+        def _():
+            pl.semaphore_signal(barrier, inc=1, device_id=peer, device_id_type=MESH)
+    fetch_r = pltpu.make_async_copy(response_hbm, response_ref, load.at[0])
+    fetch_t = pltpu.make_async_copy(traces_hbm, tland.at[me_d], load.at[1])
+    fetch_r.start()
+    fetch_t.start()
+    with jax.named_scope("barrier"):
+        hold(barrier, in_d + out_d + in_e + place)
+    for peer, below, kind in peers:
+        @pl.when(below)
+        def _():
+            pl.semaphore_signal(
+                joined.at[kind], inc=1, device_id=peer, device_id_type=MESH
+            )
+
+    part = rows_d // chunks
+    per_half = chunks // 2
+
+    def tpiece(n):
+        return pl.ds(lax.rem(n + in_e * per_half, chunks) * part, part)
+
+    def tcopy(owner, n, recv, peer, src=None):
+        piece = tpiece(n)
+        return pltpu.make_async_remote_copy(
+            src_ref=tland.at[owner, piece] if src is None else src.at[piece],
+            dst_ref=tland.at[owner, piece],
+            send_sem=sent.at[0],
+            recv_sem=recv,
+            device_id=peer,
+            device_id_type=MESH,
+        )
+
+    half = steps * shots // 2
+
+    def gcopy(owner, h, recv, peer):
+        piece = gland.at[owner, pl.ds(h * half, half)]
+        return pltpu.make_async_remote_copy(
+            src_ref=piece,
+            dst_ref=piece,
+            send_sem=sent.at[1],
+            recv_sem=recv,
+            device_id=peer,
+            device_id_type=MESH,
+        )
+
+    across = [tcopy(me_d, n, tpeer.at[n], (peer_d, me_e), traces_hbm) for n in range(chunks)]
+    beside = pltpu.make_async_remote_copy(
+        src_ref=traces_hbm, dst_ref=tland.at[me_d], send_sem=sent.at[0], recv_sem=tmate.at[0],
+        device_id=(mate_d, me_e), device_id_type=MESH,
+    )
+    side = [gcopy(me_e, h, gside.at[h], (me_d, mate_e)) for h in range(2)]
+    along = []
+    for spot in range(length):
+        n = jnp.where(low_bit == spot % 2, 0, 1) + jnp.where(high_bit == spot // 2, 0, 2)
+        n = jnp.maximum(n, 1)
+        along.append([gcopy(me_e, h, gline.at[n - 1, h], (me_d, 2 * spot + in_e)) for h in range(2)])
+
+    def launch(copies, when):
+        @pl.when(when)
+        def _():
+            for copy in copies:
+                copy.start()
+
+    launch(across, out_d == 1)
+    launch([beside], in_d == 1)
+    with jax.named_scope("fetch_r"):
+        fetch_r.wait()
+    with jax.named_scope("turn_r"):
+        gland[me_e] = lag_response(response_ref[...], lags, y_ref, w_ref)
+    launch(side, in_e == 1)
+    launch(along[0], place > 0)
+    with jax.named_scope("join_m"):
+        hold(joined.at[0], 1 - in_d)
+    launch([beside], in_d == 0)
+
+    first_z = place == 0
+    turn = [
+        jnp.where(first_z, 2 + in_d, 1),
+        jnp.where(first_z, 3 - in_d, 2),
+        jnp.where(first_z, 1, 3),
+    ]
+
+    def spot_of(n):
+        return sum(jnp.where(n == i, spots[i], 0) for i in range(length))
+
+    def own(n):
+        return 2 * spot_of(n) + in_e
+
+    def other(n):
+        return 2 * spot_of(n) + 1 - in_e
+
+    def pass_r(n, h):
+      with jax.named_scope(f"fr{h}"):
+        gcopy(own(n), h, gline.at[n - 1, h], (me_d, mate_e)).wait_recv()
+        gcopy(own(n), h, gover.at[n - 1, h], (me_d, mate_e)).start()
+
+    def pass_t(n):
+      with jax.named_scope(f"ft{n}"):
+        tcopy(peer_d, n, tpeer.at[n], (mate_d, me_e)).wait_recv()
+        tcopy(peer_d, n, tfar.at[n], (mate_d, me_e)).start()
+
+    def spread(d, i):
+        i = lax.rem(i + in_e, 2)
+        with jax.named_scope("spread"):
+            e = d * 2 + i
+            raw = tland[d, pl.ds(i * rows_e, rows_e)]
+            put(a_ref, raw.astype(jnp.float32).reshape(rows_e * rcv, samples))
+            for r in range(rcv):
+                x = get_rows(a_ref, r, rows_e, rcv).astype(jnp.bfloat16)
+                for j in range(lags):
+                    sh_ref[e, r, pl.ds(j * rows_e, rows_e), :] = delayed(x, j)
+
+    def far(i):
+      with jax.named_scope("wfar"):
+        for n in range(i * per_half, (i + 1) * per_half):
+            tcopy(far_d, n, tfar.at[n], (mate_d, me_e)).wait_recv()
+      spread(far_d, i)
+
+    def meet(n):
+      with jax.named_scope("meet"):
+        for h in range(2):
+            gcopy(other(n), h, gover.at[n - 1, h], (me_d, mate_e)).wait_recv()
+
+    def add(owners, first=False, last=False):
+        with jax.named_scope("add"):
+            held = jnp.concatenate([gland[e] for e in owners], axis=1)
+            for r in range(rcv):
+                total = jnp.dot(
+                    held,
+                    jnp.concatenate([sh_ref[e, r] for e in owners], axis=0),
+                    preferred_element_type=jnp.float32,
+                )
+                if not first:
+                    total = p_ref[r] + total
+                p_ref[r] = total
+                if last:
+                    fold(r)
+
+    def fold(r):
+        tiles = samples // LANES
+        total = [p_ref[r, pl.ds(0, shots), pl.ds(t * LANES, LANES)] for t in range(tiles)]
+        for n in range(1, steps):
+            lagged = later(
+                [p_ref[r, pl.ds(n * shots, shots), pl.ds(t * LANES, LANES)] for t in range(tiles)],
+                n * lags,
+            )
+            total = [v + w for v, w in zip(total, lagged)]
+        for t in range(tiles):
+            f_ref[t, pl.ds(r, shots, stride=rcv), :] = total[t]
+
+    with jax.named_scope("fetch_t"):
+        fetch_t.wait()
+    spread(me_d, 0)
+    spread(me_d, 1)
+    with jax.named_scope("wmate"):
+        pltpu.make_async_remote_copy(
+            src_ref=traces_hbm, dst_ref=tland.at[mate_d], send_sem=sent.at[0], recv_sem=tmate.at[0],
+            device_id=(mate_d, me_e), device_id_type=MESH,
+        ).wait_recv()
+    spread(mate_d, 0)
+    spread(mate_d, 1)
+    with jax.named_scope("join_x"):
+        hold(joined.at[1], 1 - out_d)
+        launch(across, out_d == 0)
+    with jax.named_scope("join_y"):
+        hold(joined.at[2], 1 - in_e)
+        launch(side, in_e == 0)
+
+    def join_z(n):
+        with jax.named_scope("join_z"):
+            hold(joined.at[2 + n], jnp.where(spots[n] > place, 1, 0))
+
+    for spot in range(1, length):
+        launch(along[spot], spot < place)
+    for n in range(1, length):
+        join_z(n)
+        for spot in range(1, length):
+            launch(along[spot], jnp.logical_and(spots[n] == spot, spot > place))
+    aligned = out_d == high_bit
+    pass_t(0)
+    pass_r(turn[0], 0)
+    pass_r(turn[0], 1)
+    pass_t(1)
+    pass_r(turn[1], 0)
+    pass_r(turn[1], 1)
+    spread(peer_d, 0)
+    pass_t(2)
+    pass_r(turn[2], 0)
+    pass_r(turn[2], 1)
+    far(0)
+    near = [own(0), own(1)]
+    rest = [other(0), other(1)]
+    add(near, first=True)
+    pass_t(3)
+    spread(peer_d, 1)
+    with jax.named_scope("side"):
+        for h in range(2):
+            gcopy(other(0), h, gside.at[h], (me_d, mate_e)).wait_recv()
+
+    def choose(yes, no):
+        return [jnp.where(first_z, a, b) for a, b in zip(yes, no)]
+
+    def pair(n):
+        return [own(n), other(n)]
+
+    aligned = out_d == high_bit
+    meet(turn[0])
+
+    @pl.when(aligned)
+    def _():
+        add(choose(pair(turn[0]), rest))
+
+    far(1)
+
+    @pl.when(jnp.logical_not(aligned))
+    def _():
+        add(choose(pair(turn[0]), rest))
+
+    meet(turn[1])
+    add(choose(pair(turn[1]), pair(2)))
+    meet(turn[2])
+    add(choose(rest, pair(3)), last=True)
+    with jax.named_scope("out"):
+        o_ref[...] = get(f_ref).reshape(shots, rcv, samples).astype(jnp.bfloat16)
+    with jax.named_scope("wsend"):
+        gone = tland.at[pl.ds(0, n_shot - 1)]
+        pltpu.make_async_copy(gone, gone, sent.at[0]).wait()
+        gone = gland.at[pl.ds(0, n_rcv - 1)]
+        pltpu.make_async_copy(gone, gone, sent.at[1]).wait()
+
+
+def shards(n_shot, n_rcv, response, traces):
+    shots, rows_e, taps = response.shape
+    rows_d, rcv, samples = traces.shape
+    lags = LANES // rows_e
+    fits = n_shot == 4 and n_rcv == 8 and rows_d == 2 * rows_e and lags * 8 == taps
+    if not fits or shots * (taps // lags) % WIDTH != 0:
+        return shards_general(n_shot, n_rcv, response, traces)
+    steps = taps // lags
+    chunks = 4
+    f32, bf16 = jnp.float32, jnp.bfloat16
+
+    def tiled(height, across):
+        return pltpu.VMEM((across // LANES, height, LANES), f32)
+
+    dma = pltpu.SemaphoreType.DMA
+    vmem = pl.BlockSpec(memory_space=pltpu.VMEM)
+    hbm = pl.BlockSpec(memory_space=pl.ANY)
+    y = pl.pallas_call(
+        functools.partial(predict_line, n_shot, n_rcv, lags, chunks),
+        out_shape=pltpu.VMEM((shots, rcv, samples), bf16),
+        in_specs=[hbm] * 2,
+        out_specs=vmem,
+        scratch_shapes=[
+            pltpu.VMEM(response.shape, bf16),
+            tiled(taps, shots * rows_e),
+            pltpu.VMEM((steps * shots, LANES), f32),
+            pltpu.VMEM((n_rcv, steps * shots, LANES), bf16),
+            pltpu.VMEM((n_shot, rows_d, rcv, samples), bf16),
+            tiled(rows_e * rcv, samples),
+            pltpu.VMEM((n_rcv, rcv, LANES, samples), bf16),
+            pltpu.VMEM((rcv, steps * shots, samples), f32),
+            tiled(shots * rcv, samples),
+            dma((2,)),
+            dma((2,)),
+            dma((1,)),
+            dma((chunks,)),
+            dma((chunks,)),
+            dma((n_rcv // 2 - 1, 2)),
+            dma((2,)),
+            dma((n_rcv // 2 - 1, 2)),
+            pltpu.SemaphoreType.REGULAR((n_rcv // 2 + 2,)),
+        ],
+        compiler_params=pltpu.CompilerParams(collective_id=1, has_side_effects=True),
+    )(response, traces)
+    return y
+
+
 def solution(mesh):
     placed = P("shot", "rcv", None)
     return jax.shard_map(

time: 20.9 us -> 18.2 us (0.87)
  Pallas kernels: 20.7 us -> 17.4 us
  local copies, waits for them, and re-layouts: 0 us -> 0.71 us
    pallas_call x2 -> x1, Pallas kernels: 20.7 us -> 17.4 us  [shards(): pl.pallas_call(functools.partial(predict_line, n_shot, n_rcv, lags, chunk...]
    unnamed x0 -> x1, local copies, waits for them, and re-layouts: none -> 0.71 us
where the time goes in v1:
time: 18.2 us; the launch traced here: 18.1 us
  Pallas kernels  17.4 us (96%)
  local copies, waits for them, and re-layouts  0.71 us (4%)
    pallas_call x1, Pallas kernels, shards(): pl.pallas_call(functools.partial(predict_line, n_shot, n_rcv, lags, chunk...  17.4 us
    unnamed x1, local copies, waits for them, and re-layouts  0.71 us

profile of v1, /device:TPU:0, one launch (start us, length us, event | category | flops | bytes accessed | tf_op | source)
XLA Modules:
  0.0 18.1 jit_solution(1942044064338831311)
XLA Ops:
  0.0 17.4 %shard_map.28 = bf16[32,8,512]{2,1,0:T(8,128)(2,1)S(1)} custom-call(bf16[32,16,64]{2,1,0:T(8,128)(2,1)} %response_hbm.1, bf16[32,8,512]{2,1,0:T(8,128)(2,1)} %traces_hbm.1), custom_call_target="tpu_custom_call" | custom-call | tf_op jit(solution)/shard_map/pallas_call | solution.py:679
  17.4 0.7 %copy.4 = bf16[32,8,512]{2,1,0:T(8,128)(2,1)} copy(bf16[32,8,512]{2,1,0:T(8,128)(2,1)S(1)} %shard_map.28) | data formatting | bytes 524288

commit v2 on v1

--- a/solution.py
+++ b/solution.py
@@ -394,7 +394,7 @@
 def predict_line(
     n_shot, n_rcv, lags, chunks,
     response_hbm, traces_hbm, o_ref,
-    response_ref, y_ref, w_ref, gland, tland, a_ref, sh_ref, p_ref, f_ref,
+    response_ref, y_ref, w_ref, gland, tland, a_ref, first_ref, second_ref, p_ref, f_ref,
     load, sent, tmate, tpeer, tfar, gline, gside, gover, joined,
 ):
     shots, rows_e, taps = response_ref.shape
@@ -460,10 +460,11 @@
             device_id_type=MESH,
         )
 
-    half = steps * shots // 2
+    cuts = 4
+    cut = steps * shots // cuts
 
     def gcopy(owner, h, recv, peer):
-        piece = gland.at[owner, pl.ds(h * half, half)]
+        piece = gland.at[owner, pl.ds(h * cut, cut)]
         return pltpu.make_async_remote_copy(
             src_ref=piece,
             dst_ref=piece,
@@ -473,17 +474,27 @@
             device_id_type=MESH,
         )
 
+    def whole(owner, recv):
+        return pltpu.make_async_remote_copy(
+            src_ref=gland.at[owner],
+            dst_ref=gland.at[owner],
+            send_sem=sent.at[1],
+            recv_sem=recv,
+            device_id=(me_d, mate_e),
+            device_id_type=MESH,
+        )
+
     across = [tcopy(me_d, n, tpeer.at[n], (peer_d, me_e), traces_hbm) for n in range(chunks)]
     beside = pltpu.make_async_remote_copy(
         src_ref=traces_hbm, dst_ref=tland.at[me_d], send_sem=sent.at[0], recv_sem=tmate.at[0],
         device_id=(mate_d, me_e), device_id_type=MESH,
     )
-    side = [gcopy(me_e, h, gside.at[h], (me_d, mate_e)) for h in range(2)]
+    side = [gcopy(me_e, h, gside.at[0], (me_d, mate_e)) for h in range(cuts)]
     along = []
     for spot in range(length):
         n = jnp.where(low_bit == spot % 2, 0, 1) + jnp.where(high_bit == spot // 2, 0, 2)
         n = jnp.maximum(n, 1)
-        along.append([gcopy(me_e, h, gline.at[n - 1, h], (me_d, 2 * spot + in_e)) for h in range(2)])
+        along.append([gcopy(me_e, h, gline.at[n - 1, h], (me_d, 2 * spot + in_e)) for h in range(cuts)])
 
     def launch(copies, when):
         @pl.when(when)
@@ -504,10 +515,11 @@
     launch([beside], in_d == 0)
 
     first_z = place == 0
+    swap = jnp.where(place == 2, 1, 0)
+    in_turn = [1 + swap, 2 - swap, 3]
     turn = [
-        jnp.where(first_z, 2 + in_d, 1),
-        jnp.where(first_z, 3 - in_d, 2),
-        jnp.where(first_z, 1, 3),
+        (jnp.where(first_z, 1 + k % 3, in_turn[k // cuts]), jnp.where(first_z, k // 3, k % cuts))
+        for k in range(3 * cuts)
     ]
 
     def spot_of(n):
@@ -519,47 +531,59 @@
     def other(n):
         return 2 * spot_of(n) + 1 - in_e
 
-    def pass_r(n, h):
-      with jax.named_scope(f"fr{h}"):
+    def pass_r(k):
+      with jax.named_scope(f"fr{k}"):
+        n, h = turn[k]
         gcopy(own(n), h, gline.at[n - 1, h], (me_d, mate_e)).wait_recv()
-        gcopy(own(n), h, gover.at[n - 1, h], (me_d, mate_e)).start()
+        gcopy(own(n), h, gover.at[n - 1], (me_d, mate_e)).start()
 
     def pass_t(n):
       with jax.named_scope(f"ft{n}"):
         tcopy(peer_d, n, tpeer.at[n], (mate_d, me_e)).wait_recv()
         tcopy(peer_d, n, tfar.at[n], (mate_d, me_e)).start()
 
+    def spreading(d, i):
+        raw = tland[d, pl.ds(lax.rem(i + in_e, 2) * rows_e, rows_e)]
+        put(a_ref, raw.astype(jnp.float32).reshape(rows_e * rcv, samples))
+        out_ref = second_ref if i else first_ref
+
+        def row(r):
+            x = get_rows(a_ref, r, rows_e, rcv).astype(jnp.bfloat16)
+            for j in range(lags):
+                out_ref[d, r, pl.ds(j * rows_e, rows_e), :] = delayed(x, j)
+
+        return row
+
     def spread(d, i):
-        i = lax.rem(i + in_e, 2)
         with jax.named_scope("spread"):
-            e = d * 2 + i
-            raw = tland[d, pl.ds(i * rows_e, rows_e)]
-            put(a_ref, raw.astype(jnp.float32).reshape(rows_e * rcv, samples))
+            row = spreading(d, i)
             for r in range(rcv):
-                x = get_rows(a_ref, r, rows_e, rcv).astype(jnp.bfloat16)
-                for j in range(lags):
-                    sh_ref[e, r, pl.ds(j * rows_e, rows_e), :] = delayed(x, j)
+                row(r)
 
     def far(i):
-      with jax.named_scope("wfar"):
-        for n in range(i * per_half, (i + 1) * per_half):
-            tcopy(far_d, n, tfar.at[n], (mate_d, me_e)).wait_recv()
-      spread(far_d, i)
+        with jax.named_scope("wfar"):
+            for n in range(i * per_half, (i + 1) * per_half):
+                tcopy(far_d, n, tfar.at[n], (mate_d, me_e)).wait_recv()
 
     def meet(n):
       with jax.named_scope("meet"):
-        for h in range(2):
-            gcopy(other(n), h, gover.at[n - 1, h], (me_d, mate_e)).wait_recv()
-
-    def add(owners, first=False, last=False):
+        whole(2 * spots[n] + 1 - in_e, gover.at[n - 1] if n else gside.at[0]).wait_recv()
+
+    def add(group, second, first=False, last=False, beside=None):
         with jax.named_scope("add"):
-            held = jnp.concatenate([gland[e] for e in owners], axis=1)
+            row = None if beside is None else spreading(*beside)
+            side = 1 - in_e if second else in_e
+            source = second_ref if second else first_ref
+            places = [spot_of(n) for n in group]
+            held = jnp.concatenate([gland[2 * z + side] for z in places], axis=1)
             for r in range(rcv):
                 total = jnp.dot(
                     held,
-                    jnp.concatenate([sh_ref[e, r] for e in owners], axis=0),
+                    jnp.concatenate([source[z, r] for z in places], axis=0),
                     preferred_element_type=jnp.float32,
                 )
+                if row is not None:
+                    row(r)
                 if not first:
                     total = p_ref[r] + total
                 p_ref[r] = total
@@ -589,6 +613,8 @@
         ).wait_recv()
     spread(mate_d, 0)
     spread(mate_d, 1)
+    for spot in reversed(range(1, length)):
+        launch(along[spot], spot < place)
     with jax.named_scope("join_x"):
         hold(joined.at[1], 1 - out_d)
         launch(across, out_d == 0)
@@ -600,56 +626,39 @@
         with jax.named_scope("join_z"):
             hold(joined.at[2 + n], jnp.where(spots[n] > place, 1, 0))
 
-    for spot in range(1, length):
-        launch(along[spot], spot < place)
     for n in range(1, length):
         join_z(n)
         for spot in range(1, length):
             launch(along[spot], jnp.logical_and(spots[n] == spot, spot > place))
     aligned = out_d == high_bit
+    aligned = out_d == high_bit
+
+    def half_of(early):
+        base = jnp.where(aligned == early, 0, 2)
+        return [base, base + 1]
+
     pass_t(0)
-    pass_r(turn[0], 0)
-    pass_r(turn[0], 1)
+    for k in range(6):
+        pass_r(k)
     pass_t(1)
-    pass_r(turn[1], 0)
-    pass_r(turn[1], 1)
+    for k in range(6, 9):
+        pass_r(k)
     spread(peer_d, 0)
     pass_t(2)
-    pass_r(turn[2], 0)
-    pass_r(turn[2], 1)
+    for k in range(9, 12):
+        pass_r(k)
     far(0)
-    near = [own(0), own(1)]
-    rest = [other(0), other(1)]
-    add(near, first=True)
+    add(half_of(True), False, first=True, beside=(far_d, 0))
     pass_t(3)
-    spread(peer_d, 1)
-    with jax.named_scope("side"):
-        for h in range(2):
-            gcopy(other(0), h, gside.at[h], (me_d, mate_e)).wait_recv()
-
-    def choose(yes, no):
-        return [jnp.where(first_z, a, b) for a, b in zip(yes, no)]
-
-    def pair(n):
-        return [own(n), other(n)]
-
-    aligned = out_d == high_bit
-    meet(turn[0])
-
-    @pl.when(aligned)
-    def _():
-        add(choose(pair(turn[0]), rest))
-
+    add(half_of(False), False, beside=(peer_d, 1))
     far(1)
-
-    @pl.when(jnp.logical_not(aligned))
-    def _():
-        add(choose(pair(turn[0]), rest))
-
-    meet(turn[1])
-    add(choose(pair(turn[1]), pair(2)))
-    meet(turn[2])
-    add(choose(rest, pair(3)), last=True)
+    spread(far_d, 1)
+    meet(0)
+    meet(1)
+    add([0, 1], True)
+    meet(2)
+    meet(3)
+    add([2, 3], True, last=True)
     with jax.named_scope("out"):
         o_ref[...] = get(f_ref).reshape(shots, rcv, samples).astype(jnp.bfloat16)
     with jax.named_scope("wsend"):
@@ -688,7 +697,8 @@
             pltpu.VMEM((n_rcv, steps * shots, LANES), bf16),
             pltpu.VMEM((n_shot, rows_d, rcv, samples), bf16),
             tiled(rows_e * rcv, samples),
-            pltpu.VMEM((n_rcv, rcv, LANES, samples), bf16),
+            pltpu.VMEM((n_shot, rcv, LANES, samples), bf16),
+            pltpu.VMEM((n_shot, rcv, LANES, samples), bf16),
             pltpu.VMEM((rcv, steps * shots, samples), f32),
             tiled(shots * rcv, samples),
             dma((2,)),
@@ -696,9 +706,9 @@
             dma((1,)),
             dma((chunks,)),
             dma((chunks,)),
-            dma((n_rcv // 2 - 1, 2)),
-            dma((2,)),
-            dma((n_rcv // 2 - 1, 2)),
+            dma((n_rcv // 2 - 1, 4)),
+            dma((1,)),
+            dma((n_rcv // 2 - 1,)),
             pltpu.SemaphoreType.REGULAR((n_rcv // 2 + 2,)),
         ],
         compiler_params=pltpu.CompilerParams(collective_id=1, has_side_effects=True),

time: 18.2 us -> 16.8 us (0.923)
  the two profiles are of different devices: /device:TPU:0 before, /device:TPU:9 now
where the time goes in v2:
time: 16.8 us; the launch traced here: 16.6 us
  Pallas kernels  15.9 us (95%)
  local copies, waits for them, and re-layouts  0.71 us (4%)
    pallas_call x1, Pallas kernels, shards(): pl.pallas_call(functools.partial(predict_line, n_shot, n_rcv, lags, chunk...  15.9 us
    unnamed x1, local copies, waits for them, and re-layouts  0.71 us

profile of v2, /device:TPU:9, one launch (start us, length us, event | category | flops | bytes accessed | tf_op | source)
XLA Modules:
  0.0 16.6 jit_solution(15638384354953092961)
XLA Ops:
  0.0 15.9 %shard_map.28 = bf16[32,8,512]{2,1,0:T(8,128)(2,1)S(1)} custom-call(bf16[32,16,64]{2,1,0:T(8,128)(2,1)} %response_hbm.1, bf16[32,8,512]{2,1,0:T(8,128)(2,1)} %traces_hbm.1), custom_call_target="tpu_custom_call" | custom-call | tf_op jit(solution)/shard_map/pallas_call | solution.py:688
  15.9 0.7 %copy.4 = bf16[32,8,512]{2,1,0:T(8,128)(2,1)} copy(bf16[32,8,512]{2,1,0:T(8,128)(2,1)S(1)} %shard_map.28) | data formatting | bytes 524288

commit v3 on v2

--- a/solution.py
+++ b/solution.py
@@ -535,7 +535,7 @@
       with jax.named_scope(f"fr{k}"):
         n, h = turn[k]
         gcopy(own(n), h, gline.at[n - 1, h], (me_d, mate_e)).wait_recv()
-        gcopy(own(n), h, gover.at[n - 1], (me_d, mate_e)).start()
+        gcopy(own(n), h, gover.at[h // (cuts // 2)], (me_d, mate_e)).start()
 
     def pass_t(n):
       with jax.named_scope(f"ft{n}"):
@@ -565,40 +565,49 @@
             for n in range(i * per_half, (i + 1) * per_half):
                 tcopy(far_d, n, tfar.at[n], (mate_d, me_e)).wait_recv()
 
-    def meet(n):
+    def meet(part):
       with jax.named_scope("meet"):
-        whole(2 * spots[n] + 1 - in_e, gover.at[n - 1] if n else gside.at[0]).wait_recv()
-
-    def add(group, second, first=False, last=False, beside=None):
-        with jax.named_scope("add"):
-            row = None if beside is None else spreading(*beside)
-            side = 1 - in_e if second else in_e
-            source = second_ref if second else first_ref
-            places = [spot_of(n) for n in group]
-            held = jnp.concatenate([gland[2 * z + side] for z in places], axis=1)
-            for r in range(rcv):
-                total = jnp.dot(
+        if part == 0:
+            whole(2 * place + 1 - in_e, gside.at[0]).wait_recv()
+        rows = gland.at[pl.ds(0, length - 1), pl.ds(0, steps * shots // 2)]
+        pltpu.make_async_copy(rows, rows, gover.at[part]).wait()
+
+    def gather(rows, beside):
+        with jax.named_scope("gather"):
+            row = spreading(*beside)
+            held = jnp.concatenate([gland[2 * z + in_e] for z in spots], axis=1)
+            for n, r in enumerate(rows):
+                p_ref[r] = jnp.dot(
                     held,
-                    jnp.concatenate([source[z, r] for z in places], axis=0),
+                    jnp.concatenate([first_ref[z, r] for z in spots], axis=0),
                     preferred_element_type=jnp.float32,
                 )
-                if row is not None:
-                    row(r)
-                if not first:
-                    total = p_ref[r] + total
-                p_ref[r] = total
-                if last:
-                    fold(r)
-
-    def fold(r):
+                for i in range(n * rcv // len(rows), (n + 1) * rcv // len(rows)):
+                    row(i)
+
+    def close(part):
+        with jax.named_scope("close"):
+            rows = pl.ds(part * steps * shots // 2, steps * shots // 2)
+            held = jnp.concatenate([gland[2 * z + 1 - in_e, rows] for z in spots], axis=1)
+            for r in range(rcv):
+                p_ref[r, rows] = p_ref[r, rows] + jnp.dot(
+                    held,
+                    jnp.concatenate([second_ref[z, r] for z in spots], axis=0),
+                    preferred_element_type=jnp.float32,
+                )
+                fold(r, part)
+
+    def fold(r, part):
         tiles = samples // LANES
-        total = [p_ref[r, pl.ds(0, shots), pl.ds(t * LANES, LANES)] for t in range(tiles)]
-        for n in range(1, steps):
+        total = None
+        if part > 0:
+            total = [f_ref[t, pl.ds(r, shots, stride=rcv), :] for t in range(tiles)]
+        for n in range(part * steps // 2, (part + 1) * steps // 2):
             lagged = later(
                 [p_ref[r, pl.ds(n * shots, shots), pl.ds(t * LANES, LANES)] for t in range(tiles)],
                 n * lags,
             )
-            total = [v + w for v, w in zip(total, lagged)]
+            total = lagged if total is None else [v + w for v, w in zip(total, lagged)]
         for t in range(tiles):
             f_ref[t, pl.ds(r, shots, stride=rcv), :] = total[t]
 
@@ -606,6 +615,19 @@
         fetch_t.wait()
     spread(me_d, 0)
     spread(me_d, 1)
+    with jax.named_scope("join_x"):
+        hold(joined.at[1], 1 - out_d)
+        launch(across, out_d == 0)
+    with jax.named_scope("join_y"):
+        hold(joined.at[2], 1 - in_e)
+        launch(side, in_e == 0)
+    for spot in range(1, length):
+        n = jnp.where(low_bit == spot % 2, 0, 1) + jnp.where(high_bit == spot // 2, 0, 2)
+        with jax.named_scope("join_z"):
+            hold(joined.at[2 + jnp.maximum(n, 1)], jnp.where(spot > place, 1, 0))
+        launch(along[spot], spot > place)
+    for spot in reversed(range(1, length)):
+        launch(along[spot], spot < place)
     with jax.named_scope("wmate"):
         pltpu.make_async_remote_copy(
             src_ref=traces_hbm, dst_ref=tland.at[mate_d], send_sem=sent.at[0], recv_sem=tmate.at[0],
@@ -613,52 +635,25 @@
         ).wait_recv()
     spread(mate_d, 0)
     spread(mate_d, 1)
-    for spot in reversed(range(1, length)):
-        launch(along[spot], spot < place)
-    with jax.named_scope("join_x"):
-        hold(joined.at[1], 1 - out_d)
-        launch(across, out_d == 0)
-    with jax.named_scope("join_y"):
-        hold(joined.at[2], 1 - in_e)
-        launch(side, in_e == 0)
-
-    def join_z(n):
-        with jax.named_scope("join_z"):
-            hold(joined.at[2 + n], jnp.where(spots[n] > place, 1, 0))
-
-    for n in range(1, length):
-        join_z(n)
-        for spot in range(1, length):
-            launch(along[spot], jnp.logical_and(spots[n] == spot, spot > place))
-    aligned = out_d == high_bit
-    aligned = out_d == high_bit
-
-    def half_of(early):
-        base = jnp.where(aligned == early, 0, 2)
-        return [base, base + 1]
-
     pass_t(0)
-    for k in range(6):
+    for k in range(4):
         pass_r(k)
     pass_t(1)
-    for k in range(6, 9):
+    spread(peer_d, 0)
+    for k in range(4, 9):
         pass_r(k)
-    spread(peer_d, 0)
     pass_t(2)
     for k in range(9, 12):
         pass_r(k)
+    pass_t(3)
     far(0)
-    add(half_of(True), False, first=True, beside=(far_d, 0))
-    pass_t(3)
-    add(half_of(False), False, beside=(peer_d, 1))
+    spread(far_d, 0)
+    gather(range(rcv // 2), (peer_d, 1))
     far(1)
-    spread(far_d, 1)
-    meet(0)
-    meet(1)
-    add([0, 1], True)
-    meet(2)
-    meet(3)
-    add([2, 3], True, last=True)
+    gather(range(rcv // 2, rcv), (far_d, 1))
+    for part in range(2):
+        meet(part)
+        close(part)
     with jax.named_scope("out"):
         o_ref[...] = get(f_ref).reshape(shots, rcv, samples).astype(jnp.bfloat16)
     with jax.named_scope("wsend"):
@@ -708,7 +703,7 @@
             dma((chunks,)),
             dma((n_rcv // 2 - 1, 4)),
             dma((1,)),
-            dma((n_rcv // 2 - 1,)),
+            dma((2,)),
             pltpu.SemaphoreType.REGULAR((n_rcv // 2 + 2,)),
         ],
         compiler_params=pltpu.CompilerParams(collective_id=1, has_side_effects=True),

time: 16.8 us -> 15.8 us (0.940)
  the two profiles are of different devices: /device:TPU:9 before, /device:TPU:0 now
where the time goes in v3:
time: 15.8 us; the launch traced here: 15.6 us
  Pallas kernels  14.9 us (94%)
  local copies, waits for them, and re-layouts  0.71 us (4%)
    pallas_call x1, Pallas kernels, shards(): pl.pallas_call(functools.partial(predict_line, n_shot, n_rcv, lags, chunk...  14.9 us
    unnamed x1, local copies, waits for them, and re-layouts  0.71 us

profile of v3, /device:TPU:0, one launch (start us, length us, event | category | flops | bytes accessed | tf_op | source)
XLA Modules:
  0.0 15.6 jit_solution(15055471972263737083)
XLA Ops:
  0.0 14.9 %shard_map.28 = bf16[32,8,512]{2,1,0:T(8,128)(2,1)S(1)} custom-call(bf16[32,16,64]{2,1,0:T(8,128)(2,1)} %response_hbm.1, bf16[32,8,512]{2,1,0:T(8,128)(2,1)} %traces_hbm.1), custom_call_target="tpu_custom_call" | custom-call | tf_op jit(solution)/shard_map/pallas_call | solution.py:683
  14.9 0.7 %copy.4 = bf16[32,8,512]{2,1,0:T(8,128)(2,1)} copy(bf16[32,8,512]{2,1,0:T(8,128)(2,1)S(1)} %shard_map.28) | data formatting | bytes 524288

commit v4 on v3

--- a/solution.py
+++ b/solution.py
@@ -358,30 +358,16 @@
     return rows
 
 
-def lag_response(response, lags, y_ref, w_ref):
+def lag_response(response, lags, b_ref, y_ref, w_ref):
     shots, rows_e, taps = response.shape
     per_tile = LANES // rows_e
-    flat = response.reshape(shots * rows_e, taps)
-    row = lax.broadcasted_iota(jnp.int32, (taps, taps), 0)
-    col = lax.broadcasted_iota(jnp.int32, (taps, taps), 1)
-    put(y_ref, lax.dot_general(
-        (row == col).astype(jnp.bfloat16), flat, (((1,), (1,)), ((), ())),
-        preferred_element_type=jnp.float32,
-    ))
+    b_ref[:, :taps] = response.reshape(shots * rows_e, taps).astype(jnp.float32)
     for tile in range(shots // per_tile):
+        y_ref[tile] = b_ref[pl.ds(tile * LANES, LANES), :].T[:taps]
         rows = [y_ref[tile, pl.ds(j, taps // lags, stride=lags), :] for j in range(lags)]
         for i, value in enumerate(swap_groups(rows, rows_e)):
             w_ref[pl.ds(tile * per_tile + i, taps // lags, stride=shots), :] = value
     return w_ref[...].astype(jnp.bfloat16)
-
-
-def later(tiles, lag):
-    if lag == 0:
-        return tiles
-    turned = [pltpu.roll(v, lag, 1) for v in tiles]
-    lane = lax.broadcasted_iota(jnp.int32, tiles[0].shape, 1)
-    before = [jnp.zeros_like(turned[0])] + turned[:-1]
-    return [jnp.where(lane >= lag, v, b) for v, b in zip(turned, before)]
 
 
 def delayed(x, lag):
@@ -394,7 +380,7 @@
 def predict_line(
     n_shot, n_rcv, lags, chunks,
     response_hbm, traces_hbm, o_ref,
-    response_ref, y_ref, w_ref, gland, tland, a_ref, first_ref, second_ref, p_ref, f_ref,
+    response_ref, b_ref, y_ref, w_ref, gland, tland, a_ref, first_ref, second_ref, p_ref, part_ref, f_ref,
     load, sent, tmate, tpeer, tfar, gline, gside, gover, joined,
 ):
     shots, rows_e, taps = response_ref.shape
@@ -507,7 +493,7 @@
     with jax.named_scope("fetch_r"):
         fetch_r.wait()
     with jax.named_scope("turn_r"):
-        gland[me_e] = lag_response(response_ref[...], lags, y_ref, w_ref)
+        gland[me_e] = lag_response(response_ref[...], lags, b_ref, y_ref, w_ref)
     launch(side, in_e == 1)
     launch(along[0], place > 0)
     with jax.named_scope("join_m"):
@@ -516,9 +502,19 @@
 
     first_z = place == 0
     swap = jnp.where(place == 2, 1, 0)
-    in_turn = [1 + swap, 2 - swap, 3]
+    flip = jnp.where(jnp.logical_or(place == 3, jnp.logical_and(place == 1, in_d == 1)), 1, 0)
+    in_turn = [1 + swap, 2 - swap + flip, 3 - flip]
+    mixed = [
+        (1, 0), (1, 1), (2, 0), (1, 2), (3, 0), (3, 1), (2, 1), (1, 3), (3, 2), (2, 2), (3, 3), (2, 3)
+    ]
+    late = jnp.logical_and(place == 1, in_d == 0)
+    paired = [(1, h) for h in range(cuts)]
+    paired += [(n, h) for part in range(2) for n in (2, 3) for h in (2 * part, 2 * part + 1)]
     turn = [
-        (jnp.where(first_z, 1 + k % 3, in_turn[k // cuts]), jnp.where(first_z, k // 3, k % cuts))
+        (
+            jnp.where(first_z, mixed[k][0], jnp.where(late, paired[k][0], in_turn[k // cuts])),
+            jnp.where(first_z, mixed[k][1], jnp.where(late, paired[k][1], k % cuts)),
+        )
         for k in range(3 * cuts)
     ]
 
@@ -540,7 +536,7 @@
     def pass_t(n):
       with jax.named_scope(f"ft{n}"):
         tcopy(peer_d, n, tpeer.at[n], (mate_d, me_e)).wait_recv()
-        tcopy(peer_d, n, tfar.at[n], (mate_d, me_e)).start()
+        tcopy(peer_d, n, tfar.at[n // per_half], (mate_d, me_e)).start()
 
     def spreading(d, i):
         raw = tland[d, pl.ds(lax.rem(i + in_e, 2) * rows_e, rows_e)]
@@ -562,8 +558,8 @@
 
     def far(i):
         with jax.named_scope("wfar"):
-            for n in range(i * per_half, (i + 1) * per_half):
-                tcopy(far_d, n, tfar.at[n], (mate_d, me_e)).wait_recv()
+            landed = tland.at[far_d, pl.ds(lax.rem(i + in_e, 2) * rows_e, rows_e)]
+            pltpu.make_async_copy(landed, landed, tfar.at[i]).wait()
 
     def meet(part):
       with jax.named_scope("meet"):
@@ -587,29 +583,35 @@
 
     def close(part):
         with jax.named_scope("close"):
-            rows = pl.ds(part * steps * shots // 2, steps * shots // 2)
+            count = steps // 2
+            rows = pl.ds(part * count * shots, count * shots)
             held = jnp.concatenate([gland[2 * z + 1 - in_e, rows] for z in spots], axis=1)
+            lane = lax.broadcasted_iota(jnp.int32, (shots, LANES), 1)
             for r in range(rcv):
-                p_ref[r, rows] = p_ref[r, rows] + jnp.dot(
-                    held,
-                    jnp.concatenate([second_ref[z, r] for z in spots], axis=0),
-                    preferred_element_type=jnp.float32,
-                )
-                fold(r, part)
-
-    def fold(r, part):
-        tiles = samples // LANES
-        total = None
-        if part > 0:
-            total = [f_ref[t, pl.ds(r, shots, stride=rcv), :] for t in range(tiles)]
-        for n in range(part * steps // 2, (part + 1) * steps // 2):
-            lagged = later(
-                [p_ref[r, pl.ds(n * shots, shots), pl.ds(t * LANES, LANES)] for t in range(tiles)],
-                n * lags,
-            )
-            total = lagged if total is None else [v + w for v, w in zip(total, lagged)]
-        for t in range(tiles):
-            f_ref[t, pl.ds(r, shots, stride=rcv), :] = total[t]
+                before = [0.0] * count
+                for c in range(samples // WIDTH):
+                    cols = pl.ds(c * WIDTH, WIDTH)
+                    total = p_ref[r, rows, cols] + jnp.dot(
+                        held,
+                        jnp.concatenate([second_ref[z, r, :, cols] for z in spots], axis=0),
+                        preferred_element_type=jnp.float32,
+                    )
+                    for t in range(WIDTH // LANES):
+                        at = c * WIDTH // LANES + t
+                        tile = pl.ds(at * LANES, LANES)
+                        value = None if part == 0 else part_ref[r, :, tile]
+                        for n in range(count):
+                            lag = (part * count + n) * lags
+                            x = total[n * shots : (n + 1) * shots, t * LANES : (t + 1) * LANES]
+                            if lag > 0:
+                                turned = pltpu.roll(x, lag, 1)
+                                x = jnp.where(lane >= lag, turned, before[n])
+                                before[n] = turned
+                            value = x if value is None else value + x
+                        if part == 0:
+                            part_ref[r, :, tile] = value
+                        else:
+                            f_ref[at, pl.ds(r, shots, stride=rcv), :] = value
 
     with jax.named_scope("fetch_t"):
         fetch_t.wait()
@@ -687,6 +689,7 @@
         out_specs=vmem,
         scratch_shapes=[
             pltpu.VMEM(response.shape, bf16),
+            pltpu.VMEM((shots * rows_e, LANES), f32),
             tiled(taps, shots * rows_e),
             pltpu.VMEM((steps * shots, LANES), f32),
             pltpu.VMEM((n_rcv, steps * shots, LANES), bf16),
@@ -695,12 +698,13 @@
             pltpu.VMEM((n_shot, rcv, LANES, samples), bf16),
             pltpu.VMEM((n_shot, rcv, LANES, samples), bf16),
             pltpu.VMEM((rcv, steps * shots, samples), f32),
+            pltpu.VMEM((rcv, shots, samples), f32),
             tiled(shots * rcv, samples),
             dma((2,)),
             dma((2,)),
             dma((1,)),
             dma((chunks,)),
-            dma((chunks,)),
+            dma((2,)),
             dma((n_rcv // 2 - 1, 4)),
             dma((1,)),
             dma((2,)),

time: 15.8 us -> 15.4 us (0.975)
  Pallas kernels: 14.9 us -> 14.6 us
    pallas_call x1, Pallas kernels: 14.9 us -> 14.6 us  [shards(): pl.pallas_call(functools.partial(predict_line, n_shot, n_rcv, lags, chunk...]
where the time goes in v4:
time: 15.4 us; the launch traced here: 15.3 us
  Pallas kernels  14.6 us (95%)
  local copies, waits for them, and re-layouts  0.71 us (5%)
    pallas_call x1, Pallas kernels, shards(): pl.pallas_call(functools.partial(predict_line, n_shot, n_rcv, lags, chunk...  14.6 us
    unnamed x1, local copies, waits for them, and re-layouts  0.71 us

profile of v4, /device:TPU:0, one launch (start us, length us, event | category | flops | bytes accessed | tf_op | source)
XLA Modules:
  0.0 15.3 jit_solution(1803736771443684677)
XLA Ops:
  0.0 14.6 %shard_map.28 = bf16[32,8,512]{2,1,0:T(8,128)(2,1)S(1)} custom-call(bf16[32,16,64]{2,1,0:T(8,128)(2,1)} %response_hbm.1, bf16[32,8,512]{2,1,0:T(8,128)(2,1)} %traces_hbm.1), custom_call_target="tpu_custom_call" | custom-call | tf_op jit(solution)/shard_map/pallas_call | solution.py:685
  14.6 0.7 %copy.4 = bf16[32,8,512]{2,1,0:T(8,128)(2,1)} copy(bf16[32,8,512]{2,1,0:T(8,128)(2,1)S(1)} %shard_map.28) | data formatting | bytes 524288

commit v5 on v4

--- a/solution.py
+++ b/solution.py
@@ -363,7 +363,8 @@
     per_tile = LANES // rows_e
     b_ref[:, :taps] = response.reshape(shots * rows_e, taps).astype(jnp.float32)
     for tile in range(shots // per_tile):
-        y_ref[tile] = b_ref[pl.ds(tile * LANES, LANES), :].T[:taps]
+        turned = b_ref[pl.ds(tile * LANES, LANES), :].T
+        y_ref[tile] = jnp.concatenate([turned[lags:taps], turned[:lags]])
         rows = [y_ref[tile, pl.ds(j, taps // lags, stride=lags), :] for j in range(lags)]
         for i, value in enumerate(swap_groups(rows, rows_e)):
             w_ref[pl.ds(tile * per_tile + i, taps // lags, stride=shots), :] = value
@@ -418,7 +419,10 @@
             pl.semaphore_signal(barrier, inc=1, device_id=peer, device_id_type=MESH)
     fetch_r = pltpu.make_async_copy(response_hbm, response_ref, load.at[0])
     fetch_t = pltpu.make_async_copy(traces_hbm, tland.at[me_d], load.at[1])
-    fetch_r.start()
+    share = shots // 4
+    for i in range(4):
+        some = pl.ds(i * share, share)
+        pltpu.make_async_copy(response_hbm.at[some], response_ref.at[some], load.at[0]).start()
     fetch_t.start()
     with jax.named_scope("barrier"):
         hold(barrier, in_d + out_d + in_e + place)
@@ -601,7 +605,7 @@
                         tile = pl.ds(at * LANES, LANES)
                         value = None if part == 0 else part_ref[r, :, tile]
                         for n in range(count):
-                            lag = (part * count + n) * lags
+                            lag = (part * count + n + 1) % steps * lags
                             x = total[n * shots : (n + 1) * shots, t * LANES : (t + 1) * LANES]
                             if lag > 0:
                                 turned = pltpu.roll(x, lag, 1)
@@ -630,6 +634,10 @@
         launch(along[spot], spot > place)
     for spot in reversed(range(1, length)):
         launch(along[spot], spot < place)
+    @pl.when(place == 0)
+    def _():
+        pass_r(0)
+
     with jax.named_scope("wmate"):
         pltpu.make_async_remote_copy(
             src_ref=traces_hbm, dst_ref=tland.at[mate_d], send_sem=sent.at[0], recv_sem=tmate.at[0],
@@ -638,7 +646,11 @@
     spread(mate_d, 0)
     spread(mate_d, 1)
     pass_t(0)
-    for k in range(4):
+    @pl.when(place > 0)
+    def _():
+        pass_r(0)
+
+    for k in range(1, 4):
         pass_r(k)
     pass_t(1)
     spread(peer_d, 0)

time: 15.4 us -> 15.3 us (level)
  no operation moved by 1% of the time
where the time goes in v5:
time: 15.3 us; the launch traced here: 15.2 us
  Pallas kernels  14.5 us (95%)
  local copies, waits for them, and re-layouts  0.71 us (5%)
    pallas_call x1, Pallas kernels, shards(): pl.pallas_call(functools.partial(predict_line, n_shot, n_rcv, lags, chunk...  14.5 us
    unnamed x1, local copies, waits for them, and re-layouts  0.71 us

profile of v5, /device:TPU:0, one launch (start us, length us, event | category | flops | bytes accessed | tf_op | source)
XLA Modules:
  0.0 15.2 jit_solution(12802790174534449313)
XLA Ops:
  0.0 14.5 %shard_map.28 = bf16[32,8,512]{2,1,0:T(8,128)(2,1)S(1)} custom-call(bf16[32,16,64]{2,1,0:T(8,128)(2,1)} %response_hbm.1, bf16[32,8,512]{2,1,0:T(8,128)(2,1)} %traces_hbm.1), custom_call_target="tpu_custom_call" | custom-call | tf_op jit(solution)/shard_map/pallas_call | solution.py:697
  14.5 0.7 %copy.4 = bf16[32,8,512]{2,1,0:T(8,128)(2,1)} copy(bf16[32,8,512]{2,1,0:T(8,128)(2,1)S(1)} %shard_map.28) | data formatting | bytes 524288

commit v6 on v5

--- a/solution.py
+++ b/solution.py
@@ -361,9 +361,9 @@
 def lag_response(response, lags, b_ref, y_ref, w_ref):
     shots, rows_e, taps = response.shape
     per_tile = LANES // rows_e
-    b_ref[:, :taps] = response.reshape(shots * rows_e, taps).astype(jnp.float32)
+    b_ref[:, :taps] = response.reshape(shots * rows_e, taps)
     for tile in range(shots // per_tile):
-        turned = b_ref[pl.ds(tile * LANES, LANES), :].T
+        turned = b_ref[pl.ds(tile * LANES, LANES), :].T.astype(jnp.float32)
         y_ref[tile] = jnp.concatenate([turned[lags:taps], turned[:lags]])
         rows = [y_ref[tile, pl.ds(j, taps // lags, stride=lags), :] for j in range(lags)]
         for i, value in enumerate(swap_groups(rows, rows_e)):
@@ -701,7 +701,7 @@
         out_specs=vmem,
         scratch_shapes=[
             pltpu.VMEM(response.shape, bf16),
-            pltpu.VMEM((shots * rows_e, LANES), f32),
+            pltpu.VMEM((shots * rows_e, LANES), bf16),
             tiled(taps, shots * rows_e),
             pltpu.VMEM((steps * shots, LANES), f32),
             pltpu.VMEM((n_rcv, steps * shots, LANES), bf16),

time: 15.3 us -> 15.3 us (level)
  no operation moved by 1% of the time
where the time goes in v6:
time: 15.3 us; the launch traced here: 15.2 us
  Pallas kernels  14.4 us (94%)
  local copies, waits for them, and re-layouts  0.71 us (5%)
    pallas_call x1, Pallas kernels, shards(): pl.pallas_call(functools.partial(predict_line, n_shot, n_rcv, lags, chunk...  14.4 us
    unnamed x1, local copies, waits for them, and re-layouts  0.71 us

profile of v6, /device:TPU:0, one launch (start us, length us, event | category | flops | bytes accessed | tf_op | source)
XLA Modules:
  0.0 15.2 jit_solution(5570576666033092607)
XLA Ops:
  0.0 14.4 %shard_map.28 = bf16[32,8,512]{2,1,0:T(8,128)(2,1)S(1)} custom-call(bf16[32,16,64]{2,1,0:T(8,128)(2,1)} %response_hbm.1, bf16[32,8,512]{2,1,0:T(8,128)(2,1)} %traces_hbm.1), custom_call_target="tpu_custom_call" | custom-call | tf_op jit(solution)/shard_map/pallas_call | solution.py:697
  14.4 0.7 %copy.4 = bf16[32,8,512]{2,1,0:T(8,128)(2,1)} copy(bf16[32,8,512]{2,1,0:T(8,128)(2,1)S(1)} %shard_map.28) | data formatting | bytes 524288
